TPU v7x, 32 devices: a whole 2x2x4 slice. The times are simulated.
32 devices in a mesh: member: 4 (over y, x), domain: 8 (over z, core).
Axes of the slice: x: 2, y: 2, z: 4, core: 2. Of those that a mesh axis runs over, the one named last changes fastest.
Arguments:
- ensemble: float32 [80, 4, 3, 16, 2048], P('member', None, None, None, 'domain'), may hold values from -9 to 9
- velocity: float32 [2, 3, 16, 2048], P(None, None, None, 'domain'), may hold values from -0.5 to 0.5
- diffusivity: float32 [4], replicated, may hold values from 0.05 to 0.2
- land_mask: int32 [16, 2048], P(None, 'domain'), may hold values from 0 to 1
- obs_index: int32 [4, 8, 4], replicated, may hold values from 0 to 255, as said below
- obs_owner: int32 [4], replicated, may hold values from 0 to 31, as said below
- obs_value: float32 [4, 8], replicated, may hold values from -4 to 4
- obs_error: float32 [4, 8], replicated, may hold values from 0.2 to 1
Outputs:
- analysis: float32 [80, 4, 3, 16, 2048], P(None, None, None, 'member', 'domain')
Inputs may be any that keep to these rules, and one draw needn't show every extreme that they name: `obs_index`: each observed cell has land_mask 1. The first observation of batch 0 is field 0, level 0 at its block's first row and column; the last observation of batch 3 is field 3, level 2 at its block's last row and column. A device's number is its member index times the number of domain tiles plus its domain index. obs_owner[0] is the first device and obs_owner[3] the last.
All inputs are finite; a program needn't handle non-finite values.
Results may differ from a plain program's by a relative error of at most 0.0001.
Values sent between devices are 32-bit elements; how exact they have to be, the bound alone decides.
No kernel may reach another device: no remote copies, remote signals or barrier semaphores. Data moves between devices by JAX's collectives and lax.ppermute only.
A program may use at most 192 MiB of HBM per device.

v0:
```python
import jax
import jax.numpy as jnp
from jax import lax
from jax.sharding import PartitionSpec as P

LOC_RADIUS = 64


def padded_2(array, sides, width):
    for axis, dim in sides:
        size, length = (lax.axis_size(axis), array.shape[dim])
        up = [(i, (i + 1) % size) for i in range(size)]
        down = [(j, i) for i, j in up]
        last = lax.slice_in_dim(array, length - width, length, axis=dim)
        initial = lax.slice_in_dim(array, 0, width, axis=dim)
        before = lax.ppermute(last, axis, up)
        after = lax.ppermute(initial, axis, down)
        array = jnp.concatenate([before, array, after], axis=dim)
    return array


def broadcast(value, axis, source):
    kept = jnp.where(lax.axis_index(axis) == source, value, 0).astype(value.dtype)
    return lax.psum(kept, axis)


def gaspari(distance, loc_radius):
    scaled = distance / loc_radius
    scaled_safe = jnp.maximum(scaled, 1.0)
    near_part = (
        ((-0.25 * scaled + 0.5) * scaled + 0.625) * scaled - 5.0 / 3.0
    ) * scaled * scaled + 1.0
    far_part = (
        ((((scaled / 12.0 - 0.5) * scaled + 0.625) * scaled + 5.0 / 3.0) * scaled - 5.0) * scaled
        + 4.0
        - 2.0 / (3.0 * scaled_safe)
    )
    return jnp.where(scaled <= 1.0, near_part, jnp.where(scaled < 2.0, far_part, 0.0))


def separation(row_from, col_from, row_to, col_to, grid_width):
    col_gap = jnp.abs(col_from - col_to)
    col_gap = jnp.minimum(col_gap, grid_width - col_gap)
    row_gap = row_from - row_to
    return jnp.sqrt((col_gap * col_gap + row_gap * row_gap).astype(jnp.float32))


def advance(center, col_next, col_prev, row_next, row_prev, flow_u, flow_v, diffuse, wet_part):
    tendency = (
        -flow_u * (col_next - col_prev) * 0.5
        - flow_v * (row_next - row_prev) * 0.5
        + diffuse * (col_next + col_prev + row_next + row_prev - 4.0 * center)
    )
    return wet_part * (center + tendency)


def regroup(member_state):
    return lax.all_to_all(member_state, "member", split_axis=3, concat_axis=0, tiled=True)


def increment_sums(change_flat, wet_cells, levels_total, members):
    per_cell = jnp.sum(change_flat.reshape(members, levels_total, -1), axis=0)
    local_sum = jnp.sum(per_cell * wet_cells[None, :], axis=1)
    return lax.psum((local_sum, jnp.sum(wet_cells)), ("member", "domain"))


def local(ensemble, velocity, diffusivity, land_mask, obs_index, obs_owner, obs_value, obs_error):
    fields = diffusivity.shape[0]
    levels = velocity.shape[1]
    levels_total = fields * levels
    diffuse = diffusivity[None, :, None, None, None]
    domain_count = lax.axis_size("domain")
    wet_all = land_mask.astype(jnp.float32)
    padded = padded_2(ensemble, (("domain", 4),), 1)
    zero_row = jnp.zeros_like(ensemble[:, :, :, :1, :])
    row_next = jnp.concatenate([ensemble[:, :, :, 1:, :], zero_row], axis=3)
    row_prev = jnp.concatenate([zero_row, ensemble[:, :, :, :-1, :]], axis=3)
    stepped = advance(
        ensemble,
        padded[..., 2:],
        padded[..., :-2],
        row_next,
        row_prev,
        velocity[0][None, None],
        velocity[1][None, None],
        diffuse,
        wet_all,
    )
    current = regroup(stepped)
    row_count = current.shape[3]
    first_row = lax.axis_index("member") * row_count
    wet_rows = lax.dynamic_slice_in_dim(wet_all, first_row, row_count, 0)
    members = current.shape[0]
    col_count = current.shape[4]
    grid_width = col_count * domain_count
    loc_radius = float(LOC_RADIUS)
    first_col = lax.axis_index("domain") * col_count
    grid_rows = first_row + jnp.arange(row_count, dtype=jnp.int32)[:, None]
    grid_cols = first_col + jnp.arange(col_count, dtype=jnp.int32)[None, :]
    wet_cells = wet_rows.reshape(-1)
    wet_flat = jnp.broadcast_to(wet_rows[None], (levels_total, row_count, col_count)).reshape(-1)
    flat_state = current.reshape(members, -1)
    spread = jnp.float32(members - 1)
    level_ids = jnp.arange(levels_total, dtype=jnp.int32)
    pending = jnp.zeros((levels_total,), jnp.float32)
    deferred = None
    for batch_num in range(obs_owner.shape[0]):
        obs_slot = obs_index[batch_num]
        owner_dev = obs_owner[batch_num]
        level_of = obs_slot[:, 0] * levels + obs_slot[:, 1]
        position = (level_of * row_count + obs_slot[:, 2]) * col_count + obs_slot[:, 3]
        own_priors = jnp.take(flat_state, position, axis=1).T
        priors = broadcast(own_priors, ("member", "domain"), owner_dev)
        if deferred is not None:
            total_inc, wet_count = increment_sums(deferred, wet_cells, levels_total, members)
            pending = pending + total_inc / (members * wet_count)
        lowered = jnp.sum(
            jnp.where(level_of[:, None] == level_ids[None, :], pending[None, :], 0.0), axis=1
        )
        priors = priors - lowered[:, None]
        obs_rows = owner_dev // domain_count * row_count + obs_slot[:, 2]
        obs_cols = owner_dev % domain_count * col_count + obs_slot[:, 3]
        mutual = gaspari(
            separation(
                obs_rows[:, None],
                obs_cols[:, None],
                obs_rows[None, :],
                obs_cols[None, :],
                grid_width,
            ),
            loc_radius,
        )
        before = flat_state
        for obs_num in range(priors.shape[0]):
            prior_row = priors[obs_num]
            mean_prior = jnp.mean(prior_row)
            anomaly = prior_row - mean_prior
            obs_var = obs_error[batch_num, obs_num]
            denominator = jnp.sum(anomaly * anomaly) / spread + obs_var
            shrink = 1.0 / (1.0 + jnp.sqrt(obs_var / denominator))
            weight = obs_value[batch_num, obs_num] - mean_prior - shrink * anomaly
            taper = gaspari(
                separation(grid_rows, grid_cols, obs_rows[obs_num], obs_cols[obs_num], grid_width),
                loc_radius,
            )
            taper_flat = (
                jnp.broadcast_to(taper[None], (levels_total, row_count, col_count)).reshape(-1)
                * wet_flat
            )
            covariance = jnp.dot(anomaly, flat_state, precision=lax.Precision.HIGHEST)
            kalman = taper_flat * covariance / (spread * denominator)
            flat_state = flat_state + weight[:, None] * kalman[None, :]
            prior_cov = jnp.dot(priors, anomaly, precision=lax.Precision.HIGHEST)
            priors = (
                priors
                + (mutual[obs_num] * prior_cov / (spread * denominator))[:, None] * weight[None, :]
            )
        deferred = flat_state - before
    total_inc, wet_count = increment_sums(deferred, wet_cells, levels_total, members)
    pending = pending + total_inc / (members * wet_count)
    flat_state = (
        flat_state.reshape(members, levels_total, -1)
        - pending[None, :, None] * wet_cells[None, None, :]
    ).reshape(members, -1)
    return flat_state.reshape(members, fields, levels, row_count, col_count)


def solution(mesh):
    in_specs = (
        P("member", None, None, None, "domain"),
        P(None, None, None, "domain"),
        P(),
        P(None, "domain"),
        P(),
        P(),
        P(),
        P(),
    )
    out_specs = P(None, None, None, "member", "domain")
    return jax.shard_map(local, mesh=mesh, in_specs=in_specs, out_specs=out_specs, check_vma=False)
```

profile of v0, /device:TPU:0, one launch (start us, length us, event | category | flops | bytes accessed | tf_op | source)
XLA Modules:
  0.0 1156.5 jit_solution(10798302134221968660)
XLA Ops:
  31.3 8.1 fusion.475
  100.2 12.5 %add_multiply_fusion = f32[20,4,3,16,256]{4,0,2,1,3:T(8,128)} fusion(f32[20,4,3,16,256]{4,0,2,1,3:T(8,128)} %copy.70, f32[20,4,3,15,256]{4,0,2,1,3:T(8,128)} %get-tuple-element.94, f32[20,4,3,15,256]{4,0,2,1,3:T(8,128)} %get-tuple-element.93, f32[20,4,3,16,1]{4,0,2,1,3:T(8,128)S(1)} %copy.62, f32[20,4,3,16,1]{4,0,2,1,3:T(8,128)} %copy.64, f32[4]{0:T(128)} %param.12, ...), kind=kLoop, calls=%fused_computation.6 | loop fusion | flops 17694720 | bytes 15382544 | tf_op jit(solution)/shard_map/mul | solution.py:54
  131.7 38.4 %all-to-all-done = f32[20,4,3,16,256]{4,0,2,1,3:T(8,128)} async-done(((f32[20,4,3,16,256]{4,0,2,1,3:T(8,128)}), f32[20,4,3,16,256]{4,0,2,1,3:T(8,128)}, u32[]{:S(2)}, u32[]{:S(2)}) %all-to-all-start) | async-done | bytes 3932192 | tf_op jit(solution)/shard_map/all_to_all | solution.py:58
  192.2 39.0 %psum.72 = f32[8,80]{1,0:T(8,128)S(1)} all-reduce(f32[8,80]{1,0:T(8,128)S(1)} %fusion.191), channel_id=1, replica_groups=mesh['member'=4,'domain'=8] {'member','domain'}, use_global_device_ids=true, to_apply=%region_0.0 | all-reduce | flops 640 | bytes 5120 | tf_op jit(solution)/shard_map/psum | solution.py:24
  273.1 7.2 multiply_add_fusion.33
  290.2 7.6 multiply_add_fusion.32
  307.8 7.4 multiply_add_fusion.31
  325.0 7.8 multiply_add_fusion.30
  342.9 7.6 multiply_add_fusion.29
  360.4 8.0 multiply_add_fusion.28
  378.4 8.1 multiply_add_fusion.27
  407.8 8.6 subtract_reduce_fusion.3
  419.9 40.7 %all-reduce.4 = (f32[12]{0:T(128)S(1)}, f32[]{:T(128)}, f32[8,80]{1,0:T(8,128)S(1)}) all-reduce(f32[12]{0:T(128)S(1)} %reduce_sum.726, f32[]{:T(128)} %get-tuple-element.126, f32[8,80]{1,0:T(8,128)S(1)} %fusion.190), channel_id=1, replica_groups=mesh['member'=4,'domain'=8] {'member','domain'}, use_global_device_ids=true, to_apply=%region_20.22 | all-reduce | flops 653 | bytes 5224 | tf_op jit(solution)/shard_map/psum | solution.py:64
  604.0 7.4 multiply_add_fusion.18
  621.6 8.7 multiply_add_fusion.17
  636.3 8.0 subtract_reduce_fusion.2
  648.0 40.3 %all-reduce.3 = (f32[12]{0:T(128)S(1)}, f32[8,80]{1,0:T(8,128)S(1)}) all-reduce(f32[12]{0:T(128)S(1)} %reduce_sum.747, f32[8,80]{1,0:T(8,128)S(1)} %fusion.189), channel_id=1, replica_groups=mesh['member'=4,'domain'=8] {'member','domain'}, use_global_device_ids=true, to_apply=%region_43.45 | all-reduce | flops 652 | bytes 5216 | tf_op jit(solution)/shard_map/psum | solution.py:64
  830.5 7.4 multiply_add_fusion.9
  847.9 10.9 multiply_add_fusion.8
  864.9 8.1 subtract_reduce_fusion.1
  876.8 40.4 %all-reduce.2 = (f32[12]{0:T(128)S(1)}, f32[8,80]{1,0:T(8,128)S(1)}) all-reduce(f32[12]{0:T(128)S(1)} %reduce_sum.767, f32[8,80]{1,0:T(8,128)S(1)} %fusion.188), channel_id=1, replica_groups=mesh['member'=4,'domain'=8] {'member','domain'}, use_global_device_ids=true, to_apply=%region_64.66 | all-reduce | flops 652 | bytes 5216 | tf_op jit(solution)/shard_map/psum | solution.py:64
  1061.0 7.3 multiply_add_fusion
  1092.1 40.2 %psum.80 = f32[12]{0:T(128)S(1)} all-reduce(f32[12]{0:T(128)S(1)} %reduce_sum.787), channel_id=1, replica_groups=mesh['member'=4,'domain'=8] {'member','domain'}, use_global_device_ids=true, to_apply=%region_84.86 | all-reduce | flops 12 | bytes 96 | tf_op jit(solution)/shard_map/psum | solution.py:64
  1132.5 23.8 %add_subtract_fusion = f32[80,4,3,4,256]{4,3,2,1,0:T(4,128)} fusion(f32[20,4,3,4,4,256]{5,4,2,1,0,3:T(4,128)} %copy.71, f32[4,3,4,256]{3,2,1,0:T(4,128)S(1)} %broadcast_multiply_fusion, f32[4,3,4,256]{3,2,1,0:T(4,128)S(1)} %mul.7381, f32[80]{0:T(128)S(1)} %get-tuple-element.210, f32[4,3,4,256]{3,2,1,0:T(4,128)S(1)} %mul.7348, f32[80]{0:T(128)S(1)} %fusion.266, ...), kind=kLoop, calls=%fused_computation.21 | loop fusion | flops 63897600 | bytes 9496576 | tf_op jit(solution)/shard_map/sub | solution.py:162
  (656 shorter events, 633.2 us)
Async XLA Ops:
  7.0 87.4 %collective-permute-start = (f32[20,4,3,16,1]{0,3,4,2,1:T(8,128)S(1)}, f32[20,4,3,16,1]{0,3,4,2,1:T(8,128)}, u32[]{:S(2)}, u32[]{:S(2)}) collective-permute-start(f32[20,4,3,16,1]{0,3,4,2,1:T(8,128)S(1)} %copy.76), channel_id=1, source_target_pairs={{1,0},{2,1},{3,2},{4,3},{5,4},{6,5},{7,6},{0,7},{9,8},{10,9},{11,1... | collective-permute-start | bytes 46088 | tf_op jit(solution)/shard_map/ppermute | solution.py:17
  13.6 83.1 %collective-permute-start.1 = (f32[20,4,3,16,1]{0,3,4,2,1:T(8,128)}, f32[20,4,3,16,1]{0,3,4,2,1:T(8,128)}, u32[]{:S(2)}, u32[]{:S(2)}) collective-permute-start(f32[20,4,3,16,1]{0,3,4,2,1:T(8,128)} %copy.77), channel_id=1, source_target_pairs={{0,1},{1,2},{2,3},{3,4},{4,5},{5,6},{6,7},{7,0},{8,9},{9,10},{10,1... | collective-permute-start | bytes 46088 | tf_op jit(solution)/shard_map/ppermute | solution.py:16
  31.3 32.6 %copy-start.28 = (s32[8,4]{0,1:T(4,128)}, s32[8,4]{0,1:T(4,128)S(1)}, u32[]{:S(2)}) copy-start(s32[8,4]{0,1:T(4,128)S(1)} %get-tuple-element.99) | copy-start | bytes 388
  40.1 23.8 %copy-start.18 = (s32[8,1]{0,1:T(1,128)}, s32[8,1]{0,1:T(1,128)S(1)}, u32[]{:S(2)}) copy-start(s32[8,1]{0,1:T(1,128)S(1)} %get-tuple-element.201) | copy-start | bytes 100
  42.0 21.8 %copy-start.20 = (s32[8,1]{0,1:T(1,128)}, s32[8,1]{0,1:T(1,128)S(1)}, u32[]{:S(2)}) copy-start(s32[8,1]{0,1:T(1,128)S(1)} %get-tuple-element.346) | copy-start | bytes 100
  42.0 52.3 %copy-start.22 = (s32[8,1]{0,1:T(1,128)}, s32[8,1]{0,1:T(1,128)S(1)}, u32[]{:S(2)}) copy-start(s32[8,1]{0,1:T(1,128)S(1)} %get-tuple-element.347) | copy-start | bytes 100
  42.0 52.4 %copy-start.24 = (s32[8,1]{0,1:T(1,128)}, s32[8,1]{0,1:T(1,128)S(1)}, u32[]{:S(2)}) copy-start(s32[8,1]{0,1:T(1,128)S(1)} %get-tuple-element.208) | copy-start | bytes 100
  42.0 52.4 %copy-start.26 = (s32[8,1]{0,1:T(1,128)}, s32[8,1]{0,1:T(1,128)S(1)}, u32[]{:S(2)}) copy-start(s32[8,1]{0,1:T(1,128)S(1)} %get-tuple-element.209) | copy-start | bytes 100
  112.7 13.3 %copy-start.29 = (s32[8,4]{0,1:T(4,128)S(1)}, s32[8,4]{0,1:T(4,128)}, u32[]{:S(2)}) copy-start(s32[8,4]{0,1:T(4,128)} %copy-done.28) | copy-start | bytes 388
  112.7 13.3 %copy-start.31 = (s32[8,4]{0,1:T(4,128)S(1)}, s32[8,4]{0,1:T(4,128)}, u32[]{:S(2)}) copy-start(s32[8,4]{0,1:T(4,128)} %copy-done.30) | copy-start | bytes 388
  112.7 14.4 %copy-start.15 = (f32[4,8]{1,0:T(4,128)S(1)}, f32[4,8]{1,0:T(4,128)}, u32[]{:S(2)}) copy-start(f32[4,8]{1,0:T(4,128)} %param.17) | copy-start | bytes 388
  112.7 15.1 %copy-start.16 = (f32[4,8]{1,0:T(4,128)S(1)}, f32[4,8]{1,0:T(4,128)}, u32[]{:S(2)}) copy-start(f32[4,8]{1,0:T(4,128)} %param.16) | copy-start | bytes 388
  112.8 17.3 %copy-start.25 = (s32[8,1]{0,1:T(1,128)S(1)}, s32[8,1]{0,1:T(1,128)}, u32[]{:S(2)}) copy-start(s32[8,1]{0,1:T(1,128)} %copy-done.24) | copy-start | bytes 100
  112.8 17.3 %copy-start.27 = (s32[8,1]{0,1:T(1,128)S(1)}, s32[8,1]{0,1:T(1,128)}, u32[]{:S(2)}) copy-start(s32[8,1]{0,1:T(1,128)} %copy-done.26) | copy-start | bytes 100
  112.8 17.4 %copy-start.21 = (s32[8,1]{0,1:T(1,128)S(1)}, s32[8,1]{0,1:T(1,128)}, u32[]{:S(2)}) copy-start(s32[8,1]{0,1:T(1,128)} %copy-done.20) | copy-start | bytes 100
  112.8 17.4 %copy-start.23 = (s32[8,1]{0,1:T(1,128)S(1)}, s32[8,1]{0,1:T(1,128)}, u32[]{:S(2)}) copy-start(s32[8,1]{0,1:T(1,128)} %copy-done.22) | copy-start | bytes 100
  112.8 17.6 %copy-start.19 = (s32[8,1]{0,1:T(1,128)S(1)}, s32[8,1]{0,1:T(1,128)}, u32[]{:S(2)}) copy-start(s32[8,1]{0,1:T(1,128)} %copy-done.18) | copy-start | bytes 100
  112.8 18.3 %copy-start.36 = (f32[4,256]{1,0:T(4,128)S(1)}, f32[4,256]{1,0:T(4,128)}, u32[]{:S(2)}) copy-start(f32[4,256]{1,0:T(4,128)} %get-tuple-element.103) | copy-start | bytes 12292
  112.8 18.3 %copy-start.35 = (f32[4,256]{1,0:T(4,128)S(1)}, f32[4,256]{1,0:T(4,128)}, u32[]{:S(2)}) copy-start(f32[4,256]{1,0:T(4,128)} %get-tuple-element.15) | copy-start | bytes 12292
  112.8 57.3 %all-to-all-start = ((f32[20,4,3,16,256]{4,0,2,1,3:T(8,128)}), f32[20,4,3,16,256]{4,0,2,1,3:T(8,128)}, u32[]{:S(2)}, u32[]{:S(2)}) async-start(f32[20,4,3,16,256]{4,0,2,1,3:T(8,128)} %add_multiply_fusion), calls=%async_computation | async-start | bytes 9437184 | tf_op jit(solution)/shard_map/all_to_all | solution.py:58
  407.8 53.6 %copy-start.47 = (s32[8]{0:T(128)S(1)}, s32[8]{0:T(128)}, u32[]{:S(2)}) copy-start(s32[8]{0:T(128)} %get-tuple-element.348) | copy-start | bytes 100
  636.3 52.0 %copy-start.46 = (s32[8]{0:T(128)S(1)}, s32[8]{0:T(128)}, u32[]{:S(2)}) copy-start(s32[8]{0:T(128)} %get-tuple-element.202) | copy-start | bytes 100
  864.9 52.2 %copy-start.45 = (s32[8]{0:T(128)S(1)}, s32[8]{0:T(128)}, u32[]{:S(2)}) copy-start(s32[8]{0:T(128)} %get-tuple-element.199) | copy-start | bytes 100
  864.9 57.2 %copy-start.43 = (f32[8,8]{1,0:T(8,128)S(1)}, f32[8,8]{1,0:T(8,128)}, u32[]{:S(2)}) copy-start(f32[8,8]{1,0:T(8,128)} %fusion.166) | copy-start | bytes 772
  (27 other events, 230.9 us)
where the time goes:
time: 1170 us; the launch traced here: 1160 us
  other arithmetic  365 us (31%)
  local copies, waits for them, and re-layouts  289 us (25%)
  blocking collectives  200 us (17%)
  matrix products  134 us (11%)
  between operations  120 us (10%)
  waiting for transfers between devices  38.4 us (3%)
    add x31, other arithmetic, local(): flat_state = flat_state + weight[:, None] * kalman[None, :]  203 us
    add x34, local copies, waits for them, and re-layouts, local(): flat_state = flat_state + weight[:, None] * kalman[None, :]  198 us
    psum x4, blocking collectives, increment_sums(): return lax.psum((local_sum, jnp.sum(wet_cells)), ('member', 'domain'))  162 us
    dot_general x32, matrix products, local(): covariance = jnp.dot(anomaly, flat_state, precision=lax.Precision.HIGHEST)  130 us
    mul x56, other arithmetic, separation(): return jnp.sqrt((col_gap * col_gap + row_gap * row_gap).astype(jnp.float32))  40.8 us
    psum x1, blocking collectives, broadcast(): return lax.psum(kept, axis)  39 us
    all_to_all x1, waiting for transfers between devices, regroup(): lax.all_to_all(member_state, 'member', split_axis=3, concat_axis=0, tiled...  38.4 us
    reduce_sum x4, other arithmetic, increment_sums(): per_cell = jnp.sum(change_flat.reshape(members, levels_total, -1), axis=0)  31.6 us
  transfers between devices with their start and end apart: 3, of which 1 were waited for; matrix products, arithmetic and copies ran while one was open for 7% of the time, Pallas kernels for 0%

commit v1 on v0

--- a/solution.py
+++ b/solution.py
@@ -55,7 +55,12 @@
 
 
 def regroup(member_state):
-    return lax.all_to_all(member_state, "member", split_axis=3, concat_axis=0, tiled=True)
+    return jnp.concatenate(
+        lax.all_to_all(
+            jnp.stack(jnp.split(member_state, lax.axis_size("member"), axis=3)), "member", 0, 0
+        ),
+        axis=0,
+    )
 
 
 def increment_sums(change_flat, wet_cells, levels_total, members):

time: 1170 us -> 1120 us (0.957)
  local copies, waits for them, and re-layouts: 289 us -> 267 us
  other arithmetic: 365 us -> 349 us
    add x31, other arithmetic: 203 us -> 189 us  [local(): flat_state = flat_state + weight[:, None] * kalman[None, :]]
    all_to_all x2 -> x0, local copies, waits for them, and re-layouts: 13.6 us -> none  [regroup(): lax.all_to_all(member_state, 'member', split_axis=3, concat_axis=0, tiled...]
    another operation x0 -> x3, local copies, waits for them, and re-layouts: none -> 12.8 us  [the longest x2 11.7 us: local(): flat_state = current.reshape(members, -1)]
    reshape x2 -> x0, local copies, waits for them, and re-layouts: 11.8 us -> none  [local(): flat_state = current.reshape(members, -1)]
where the time goes in v1:
time: 1120 us; the launch traced here: 1110 us
  other arithmetic  349 us (31%)
  local copies, waits for them, and re-layouts  267 us (24%)
  blocking collectives  201 us (18%)
  matrix products  134 us (12%)
  between operations  120 us (11%)
  waiting for transfers between devices  30.6 us (3%)
    add x34, local copies, waits for them, and re-layouts, local(): flat_state = flat_state + weight[:, None] * kalman[None, :]  198 us
    add x31, other arithmetic, local(): flat_state = flat_state + weight[:, None] * kalman[None, :]  189 us
    psum x4, blocking collectives, increment_sums(): return lax.psum((local_sum, jnp.sum(wet_cells)), ('member', 'domain'))  161 us
    dot_general x32, matrix products, local(): covariance = jnp.dot(anomaly, flat_state, precision=lax.Precision.HIGHEST)  130 us
    mul x56, other arithmetic, separation(): return jnp.sqrt((col_gap * col_gap + row_gap * row_gap).astype(jnp.float32))  40.5 us
    psum x1, blocking collectives, broadcast(): return lax.psum(kept, axis)  39.5 us
    reduce_sum x4, other arithmetic, increment_sums(): per_cell = jnp.sum(change_flat.reshape(members, levels_total, -1), axis=0)  31.1 us
    all_to_all x1, waiting for transfers between devices, regroup(): lax.all_to_all(jnp.stack(jnp.split(member_state, lax.axis_size('member'),...  30.6 us
  transfers between devices with their start and end apart: 3, of which 1 were waited for; matrix products, arithmetic and copies ran while one was open for 7% of the time, Pallas kernels for 0%

profile of v1, /device:TPU:0, one launch (start us, length us, event | category | flops | bytes accessed | tf_op | source)
XLA Modules:
  0.0 1110.8 jit_solution(11982151405236438053)
XLA Ops:
  19.8 7.9 fusion.476
  90.6 9.6 add_multiply_fusion
  121.8 30.6 %all-to-all-done = f32[4,20,4,3,4,256]{5,4,3,2,1,0:T(4,128)} async-done(((f32[4,20,4,3,4,256]{5,4,3,2,1,0:T(4,128)}), f32[4,20,4,3,4,256]{5,4,3,2,1,0:T(4,128)}, u32[]{:S(2)}, u32[]{:S(2)}) %all-to-all-start) | async-done | bytes 3932192 | tf_op jit(solution)/shard_map/all_to_all | solution.py:59
  167.5 39.5 %psum.72 = f32[8,80]{1,0:T(8,128)S(1)} all-reduce(f32[8,80]{1,0:T(8,128)S(1)} %fusion.191), channel_id=1, replica_groups=mesh['member'=4,'domain'=8] {'member','domain'}, use_global_device_ids=true, to_apply=%region_0.0 | all-reduce | flops 640 | bytes 5120 | tf_op jit(solution)/shard_map/psum | solution.py:24
  316.0 6.1 add.4295
  326.2 6.8 multiply_add_fusion.28
  342.8 7.3 multiply_add_fusion.27
  371.5 8.1 subtract_reduce_fusion.3
  383.1 40.3 %all-reduce.4 = (f32[12]{0:T(128)S(1)}, f32[]{:T(128)}, f32[8,80]{1,0:T(8,128)S(1)}) all-reduce(f32[12]{0:T(128)S(1)} %reduce_sum.726, f32[]{:T(128)} %get-tuple-element.130, f32[8,80]{1,0:T(8,128)S(1)} %fusion.190), channel_id=1, replica_groups=mesh['member'=4,'domain'=8] {'member','domain'}, use_global_device_ids=true, to_apply=%region_20.22 | all-reduce | flops 653 | bytes 5224 | tf_op jit(solution)/shard_map/psum | solution.py:69
  549.3 6.8 multiply_add_fusion.19
  565.9 7.3 multiply_add_fusion.18
  583.2 8.7 multiply_add_fusion.17
  598.0 8.1 subtract_reduce_fusion.2
  609.7 40.6 %all-reduce.3 = (f32[12]{0:T(128)S(1)}, f32[8,80]{1,0:T(8,128)S(1)}) all-reduce(f32[12]{0:T(128)S(1)} %reduce_sum.747, f32[8,80]{1,0:T(8,128)S(1)} %fusion.189), channel_id=1, replica_groups=mesh['member'=4,'domain'=8] {'member','domain'}, use_global_device_ids=true, to_apply=%region_43.45 | all-reduce | flops 652 | bytes 5216 | tf_op jit(solution)/shard_map/psum | solution.py:69
  775.1 6.8 multiply_add_fusion.10
  791.7 7.4 multiply_add_fusion.9
  809.3 10.9 multiply_add_fusion.8
  826.4 8.1 subtract_reduce_fusion.1
  838.2 40.3 %all-reduce.2 = (f32[12]{0:T(128)S(1)}, f32[8,80]{1,0:T(8,128)S(1)}) all-reduce(f32[12]{0:T(128)S(1)} %reduce_sum.767, f32[8,80]{1,0:T(8,128)S(1)} %fusion.188), channel_id=1, replica_groups=mesh['member'=4,'domain'=8] {'member','domain'}, use_global_device_ids=true, to_apply=%region_64.66 | all-reduce | flops 652 | bytes 5216 | tf_op jit(solution)/shard_map/psum | solution.py:69
  1005.5 6.8 multiply_add_fusion.1
  1022.1 7.3 multiply_add_fusion
  1039.2 7.0 subtract_reduce_fusion
  1046.4 40.0 %psum.80 = f32[12]{0:T(128)S(1)} all-reduce(f32[12]{0:T(128)S(1)} %reduce_sum.787), channel_id=1, replica_groups=mesh['member'=4,'domain'=8] {'member','domain'}, use_global_device_ids=true, to_apply=%region_84.86 | all-reduce | flops 12 | bytes 96 | tf_op jit(solution)/shard_map/psum | solution.py:69
  1086.6 24.0 %add_subtract_fusion = f32[80,4,3,4,256]{4,3,2,1,0:T(4,128)} fusion(f32[4,20,4,3,4,256]{5,4,3,2,1,0:T(4,128)} %all-to-all-done, f32[4,3,4,256]{3,2,1,0:T(4,128)S(1)} %broadcast_multiply_fusion, f32[4,3,4,256]{3,2,1,0:T(4,128)S(1)} %mul.7381, f32[80]{0:T(128)S(1)} %get-tuple-element.214, f32[4,3,4,256]{3,2,1,0:T(4,128)S(1)} %mul.7348, f32[80]{0:T(128)S(1)} %fusion.266, ...), kind=kLoop, calls=%fused_computation.21 | loop fusion | flops 63897600 | bytes 9496576 | tf_op jit(solution)/shard_map/sub | solution.py:167
  (604 shorter events, 604.7 us)
Async XLA Ops:
  4.1 10.3 copy-start.17
  7.6 76.0 %collective-permute-start = (f32[20,4,3,16,1]{0,3,4,2,1:T(8,128)}, f32[20,4,3,16,1]{0,3,4,2,1:T(8,128)}, u32[]{:S(2)}, u32[]{:S(2)}) collective-permute-start(f32[20,4,3,16,1]{0,3,4,2,1:T(8,128)} %copy.32), channel_id=1, source_target_pairs={{1,0},{2,1},{3,2},{4,3},{5,4},{6,5},{7,6},{0,7},{9,8},{10,9},{11,1... | collective-permute-start | bytes 46088 | tf_op jit(solution)/shard_map/ppermute | solution.py:17
  14.1 72.5 %collective-permute-start.1 = (f32[20,4,3,16,1]{0,3,4,2,1:T(8,128)}, f32[20,4,3,16,1]{0,3,4,2,1:T(8,128)}, u32[]{:S(2)}, u32[]{:S(2)}) collective-permute-start(f32[20,4,3,16,1]{0,3,4,2,1:T(8,128)} %copy.33), channel_id=1, source_target_pairs={{0,1},{1,2},{2,3},{3,4},{4,5},{5,6},{6,7},{7,0},{8,9},{9,10},{10,1... | collective-permute-start | bytes 46088 | tf_op jit(solution)/shard_map/ppermute | solution.py:16
  19.8 13.5 %copy-start.16 = (s32[4,8,4]{1,2,0:T(4,128)S(1)}, s32[4,8,4]{1,2,0:T(4,128)}, u32[]{:S(2)}) copy-start(s32[4,8,4]{1,2,0:T(4,128)} %param.14) | copy-start | bytes 1540
  19.8 13.5 %copy-start.9 = (f32[2,3,16,256]{3,2,1,0:T(8,128)S(1)}, f32[2,3,16,256]{3,2,1,0:T(8,128)}, u32[]{:S(2)}) copy-start(f32[2,3,16,256]{3,2,1,0:T(8,128)} %param.11) | copy-start | bytes 294916
  19.8 13.5 %copy-start.10 = (s32[16,256]{1,0:T(8,128)S(1)}, s32[16,256]{1,0:T(8,128)}, u32[]{:S(2)}) copy-start(s32[16,256]{1,0:T(8,128)} %param.13) | copy-start | bytes 49156
  33.3 11.7 %copy-start.14 = (s32[8,4]{0,1:T(4,128)}, s32[8,4]{0,1:T(4,128)S(1)}, u32[]{:S(2)}) copy-start(s32[8,4]{0,1:T(4,128)S(1)} %get-tuple-element.105) | copy-start | bytes 388
  103.8 5.0 copy-start.13
  103.8 12.2 %copy-start.15 = (s32[8,4]{0,1:T(4,128)S(1)}, s32[8,4]{0,1:T(4,128)}, u32[]{:S(2)}) copy-start(s32[8,4]{0,1:T(4,128)} %copy-done.14) | copy-start | bytes 388
  103.8 13.5 %copy-start.7 = (f32[4,8]{1,0:T(4,128)S(1)}, f32[4,8]{1,0:T(4,128)}, u32[]{:S(2)}) copy-start(f32[4,8]{1,0:T(4,128)} %param.17) | copy-start | bytes 388
  103.8 14.2 %copy-start.8 = (f32[4,8]{1,0:T(4,128)S(1)}, f32[4,8]{1,0:T(4,128)}, u32[]{:S(2)}) copy-start(f32[4,8]{1,0:T(4,128)} %param.16) | copy-start | bytes 388
  103.8 17.4 %copy-start.12 = (f32[4,256]{1,0:T(4,128)S(1)}, f32[4,256]{1,0:T(4,128)}, u32[]{:S(2)}) copy-start(f32[4,256]{1,0:T(4,128)} %get-tuple-element.107) | copy-start | bytes 12292
  103.8 17.4 %copy-start.11 = (f32[4,256]{1,0:T(4,128)S(1)}, f32[4,256]{1,0:T(4,128)}, u32[]{:S(2)}) copy-start(f32[4,256]{1,0:T(4,128)} %get-tuple-element.15) | copy-start | bytes 12292
  103.8 48.6 %all-to-all-start = ((f32[4,20,4,3,4,256]{5,4,3,2,1,0:T(4,128)}), f32[4,20,4,3,4,256]{5,4,3,2,1,0:T(4,128)}, u32[]{:S(2)}, u32[]{:S(2)}) async-start(f32[4,20,4,3,4,256]{5,4,3,2,1,0:T(4,128)} %pad_maximum_fusion.2), calls=%async_computation | async-start | bytes 7864320 | tf_op jit(solution)/shard_map/all_to_all | solution.py:59
  371.5 52.7 %copy-start.22 = (s32[8]{0:T(128)S(1)}, s32[8]{0:T(128)}, u32[]{:S(2)}) copy-start(s32[8]{0:T(128)} %get-tuple-element.350) | copy-start | bytes 100
  598.0 52.3 %copy-start.21 = (s32[8]{0:T(128)S(1)}, s32[8]{0:T(128)}, u32[]{:S(2)}) copy-start(s32[8]{0:T(128)} %get-tuple-element.206) | copy-start | bytes 100
  826.3 11.7 %copy-start.19 = (pred[8]{0:T(512)(128)(4,1)S(1)}, pred[8]{0:T(512)(128)(4,1)}, u32[]{:S(2)}) copy-start(pred[8]{0:T(512)(128)(4,1)} %get-tuple-element.31) | copy-start | bytes 28
  826.3 11.8 %copy-start = (f32[12,2,4,128]{3,2,1,0:T(4,128)S(1)}, f32[12,2,4,128]{3,2,1,0:T(4,128)}, u32[]{:S(2)}) copy-start(f32[12,2,4,128]{3,2,1,0:T(4,128)} %broadcast_bitcast_fusion) | copy-start | bytes 147460
  826.3 52.2 %copy-start.20 = (s32[8]{0:T(128)S(1)}, s32[8]{0:T(128)}, u32[]{:S(2)}) copy-start(s32[8]{0:T(128)} %get-tuple-element.203) | copy-start | bytes 100
  826.4 57.1 %copy-start.18 = (f32[8,8]{1,0:T(8,128)S(1)}, f32[8,8]{1,0:T(8,128)}, u32[]{:S(2)}) copy-start(f32[8,8]{1,0:T(8,128)} %fusion.166) | copy-start | bytes 772
  924.5 4.1 copy-start.6
  939.6 4.1 copy-start.5
  955.3 4.1 copy-start.4
  1001.3 4.1 copy-start.1
  (2 other events, 8.1 us)
